TPU v7x, 256 devices: a whole 4x4x8 slice. The times are simulated.
256 devices in a mesh: snap: 4 (over x_hi, core), param: 64 (over x_lo, z, y).
Axes of the slice: x: 4 (x_hi: 2, x_lo: 2; x = x_hi * 2 + x_lo), y: 4, z: 8, core: 2. Of those that a mesh axis runs over, the one named last changes fastest.
Arguments:
- snap_in: float32 [32, 64, 1344], P('snap', None, 'param'), may hold values from -6 to 6
- snap_qkv: float32 [32, 1344, 4032], P('snap', 'param'), may hold values from -16 to 16
- snap_proj: float32 [32, 1344, 1344], P('snap', 'param'), may hold values from -16 to 16
- snap_out: float32 [32, 1344, 64], P('snap', 'param'), may hold values from -48 to 48
- coeffs: float32 [32, 8], P('snap'), may hold values from -3 to 3
- latent: float32 [64, 64, 256], P('param'), may hold values from -6 to 6
- levels: int32 [64], P('param'), may hold values from 0 to 15
Outputs:
- denoised: float32 [8, 64, 64, 256], P('snap', 'param')
All inputs are finite; a program needn't handle non-finite values.
Results may differ from a plain program's by a relative error of at most 0.012.
Values may be sent and summed in bfloat16 or wider, within the bound.
No kernel may reach another device: no remote copies, remote signals or barrier semaphores. Data moves between devices by JAX's collectives and lax.ppermute only.
A program may use at most 192 MiB of HBM per device.

v0:
```python
import jax
import jax.numpy as jnp
from jax import lax
from jax.sharding import Mesh, PartitionSpec as P

HEAD_DIM = 64
PROF = 8
NLEV = 16
EPS = 0.0001
SNAP = ("xh", "core")
PARAM = ("xl", "z", "y")
ZY = ("z", "y")
X = ("xh", "xl")


def noise_scales(levels):
    step = levels.astype(jnp.float32) / (NLEV - 1)
    sigma = jnp.exp(jnp.log(0.2) + step * (jnp.log(5.0) - jnp.log(0.2)))
    square = sigma * sigma + 0.25
    return (1.0 / jnp.sqrt(square), 0.25 / square, 0.5 * sigma / jnp.sqrt(square))


def to_tokens(image):
    return image.reshape(16, 4, 16, 4, 4).transpose(0, 2, 1, 3, 4).reshape(256, 64)


def from_tokens(feature):
    count = feature.shape[0]
    parts = feature.reshape(count, 16, 16, 4, 4, 4).transpose(0, 1, 3, 2, 4, 5)
    return parts.reshape(count, 64, 256)


def a2a(x, axis):
    return lax.all_to_all(x, axis, 0, 0, tiled=True)


def natural(rows):
    rows = rows.reshape(32, 2, 24, 64)[:, :, :21]
    return rows.transpose(1, 0, 2, 3).reshape(1344, 64)


def shards(snap_in, snap_qkv, snap_proj, snap_out, coeffs, latent, levels):
    f32, bf16 = (jnp.float32, jnp.bfloat16)
    mix = coeffs.reshape(8, 2, 2, 2).transpose(2, 1, 3, 0).reshape(8, 8)
    eye = jnp.eye(24, 21, dtype=f32)
    mix = (mix[:, None, None, :] * eye[None, :, :, None]).reshape(192, 168)

    def contract(x):
        return jnp.dot(mix, x, precision=lax.Precision.HIGHEST).astype(bf16)

    w_q = contract(snap_qkv.transpose(1, 0, 2).reshape(168, 4032))
    w_p = contract(snap_proj.transpose(1, 0, 2).reshape(168, 1344))
    w_o = contract(snap_out.transpose(1, 0, 2).reshape(168, 64))
    w_i = contract(snap_in.transpose(2, 0, 1).reshape(168, 64))
    pad = jnp.zeros((192, 64), bf16)
    part = jnp.concatenate([w_q, pad, w_p, pad, w_i, w_o], axis=1)
    part = a2a(part.reshape(2, 96, 5632), "core").astype(f32)
    part = (part[0] + part[1]).astype(bf16)
    part = a2a(part.reshape(4, 24, 5632), X).astype(f32)
    part = part.reshape(2, 48, 5632)
    total = part[0] + part[1]
    q, p, wi, wo = (total[:, :4096], total[:, 4096:5440], total[:, 5504:5568], total[:, 5568:])
    wi = wi / (EPS + jnp.sqrt(jnp.sum(wi * wi, axis=1, keepdims=True)))
    ww = jnp.concatenate([wi, wo], axis=1).astype(bf16)
    squares = jnp.pad(jnp.sum(p * p, axis=0), (0, 64)).reshape(11, 128)
    squares = jnp.pad(squares, ((0, 5), (0, 0))).astype(bf16)
    q = q.astype(bf16).reshape(48, 32, 128).transpose(1, 0, 2)
    same = jnp.concatenate([ww, squares], axis=0)
    send = jnp.concatenate([q, jnp.broadcast_to(same[None], (32, 64, 128))], axis=1)
    got = a2a(send, ZY)
    q = got[:, :48].reshape(1536, 128)
    wi = got[:, 48:96, :64].reshape(1536, 64)
    wo = natural(got[:, 48:96, 64:])
    qf = q.astype(f32)
    qn = 1.0 / (EPS + jnp.sqrt(jnp.sum(qf * qf, axis=0)))
    m = lax.dot_general(wi, q, (((0,), (0,)), ((), ())), preferred_element_type=f32) * qn
    of = wo.astype(f32)
    on = 1.0 / (EPS + jnp.sqrt(jnp.sum(of * of, axis=0)))
    squares = jnp.sum(got[:, 96:107].astype(f32), axis=0).reshape(1408)[:1344]
    p = (p / (EPS + jnp.sqrt(squares))).astype(bf16)
    r = jnp.dot(p, wo, preferred_element_type=f32) * on
    n = (
        lax.dot_general(
            natural(got[:, 48:96, :64]), wo, (((0,), (0,)), ((), ())), preferred_element_type=f32
        )
        * on
    )
    r = r.reshape(2, 24, 64).transpose(1, 0, 2).reshape(24, 128)
    send = jnp.concatenate([m, r], axis=0).astype(bf16)
    got = a2a(jnp.broadcast_to(send[None], (32, 88, 128)), ZY)
    m = got[:, :64].transpose(1, 0, 2).reshape(64, 4096)[:, :4032]
    r = natural(got[:, 64:].reshape(32, 24, 2, 64).transpose(0, 2, 1, 3))
    c_in, c_skip, c_out = noise_scales(levels)
    tokens = to_tokens(c_in[:, None, None] * latent).astype(bf16)
    tokens = lax.all_gather(tokens, "xl", axis=0, tiled=True)
    qkv = jnp.dot(tokens, m, preferred_element_type=f32).reshape(2, 256, 3, 21, 64)
    scale = jnp.sqrt(jnp.mean(qkv * qkv, axis=-1, keepdims=True))
    qkv = (qkv / (EPS + scale)).astype(bf16)
    query, keys, values = (qkv[:, :, 0], qkv[:, :, 1], qkv[:, :, 2])
    scores = jnp.einsum("bqhd,bkhd->bhqk", query, keys, preferred_element_type=f32)
    expo = jnp.exp(scores * (1.0 / jnp.sqrt(float(HEAD_DIM))))
    weights = (expo / jnp.sum(expo, axis=-1, keepdims=True)).astype(bf16)
    attended = jnp.einsum("bhqk,bkhd->bqhd", weights, values, preferred_element_type=f32)
    attended = attended.astype(bf16).reshape(512, 1344)
    feature = 0.3 * jnp.dot(attended, r, preferred_element_type=f32)
    feature = feature + 0.7 * jnp.dot(tokens, n.astype(bf16), preferred_element_type=f32)
    feature = feature * (1.0 / jnp.sqrt(0.58))
    feature = a2a(feature.reshape(2, 256, 64), "xl")
    image = from_tokens(feature)
    out = c_skip[:, None, None] * latent + c_out[:, None, None] * image
    return out[:, None]


def solution(mesh):
    fine = Mesh(mesh.devices.reshape(2, 2, 2, 8, 4), ("xh", "core", "xl", "z", "y"))
    in_specs = (
        P(SNAP, None, PARAM),
        P(SNAP, PARAM, None),
        P(SNAP, PARAM, None),
        P(SNAP, PARAM, None),
        P(SNAP, None),
        P(PARAM, None, None),
        P(PARAM),
    )
    out_specs = P(SNAP, PARAM, None, None)
    return jax.shard_map(shards, mesh=fine, in_specs=in_specs, out_specs=out_specs, check_vma=False)
```

profile of v0, /device:TPU:8, one launch (start us, length us, event | category | flops | bytes accessed | tf_op | source)
XLA Modules:
  0.0 165.2 jit_solution(15831513101341045576)
XLA Ops:
  2.0 1.3 mul.172
  4.7 1.3 convolution_convert_fusion.3
  6.7 2.3 %convolution_convert_fusion.1 = bf16[192,1344]{1,0:T(8,128)(2,1)S(1)} fusion(f32[192,168]{0,1:T(8,128)S(1)} %mul.172, f32[8,21,1344]{2,0,1:T(8,128)} %param.9), kind=kOutput, calls=%fused_computation.9 | convolution fusion | flops 520482816 | bytes 1548288 | tf_op jit(solution)/shard_map/dot_general | solution.py:49
  9.0 3.9 %convolution_convert_fusion = bf16[192,4032]{1,0:T(8,128)(2,1)} fusion(f32[192,168]{0,1:T(8,128)S(1)} %mul.172, f32[8,21,4032]{2,0,1:T(8,128)S(1)} %copy-done), kind=kOutput, calls=%fused_computation.7 | convolution fusion | flops 1561448448 | bytes 4386816 | tf_op jit(solution)/shard_map/dot_general | solution.py:49
  12.9 4.4 %concatenate.23 = bf16[192,5632]{1,0:T(8,128)(2,1)} concatenate(bf16[192,4032]{1,0:T(8,128)(2,1)} %convolution_convert_fusion, bf16[192,64]{1,0:T(8,128)(2,1)S(1)} %broadcast_in_dim.6, bf16[192,1344]{1,0:T(8,128)(2,1)S(1)} %convolution_convert_fusion.1, bf16[192,64]{1,0:T(8,128)(2,1)S(1)} %broadcast_in_dim.6, bf16[192,64]{1,0:T(8,128)(2,1)} %copy.78, bf16[192,64]{1,0:T(8,128)(2,1)S(1)} %copy.79), dimensions={1} | concatenate | bytes 4325376 | tf_op jit(solution)/shard_map/concatenate | solution.py:56
  17.3 6.7 %all_to_all.25 = bf16[2,96,5632]{2,1,0:T(8,128)(2,1)S(1)} all-to-all(bf16[2,96,5632]{2,1,0:T(8,128)(2,1)} %bitcast.137), channel_id=1, replica_groups=mesh['xh'=2,'core'=2,'xl'=2,'z'=8,'y'=4] {'core'}, dimensions={0} | all-to-all | bytes 4325376 | tf_op jit(solution)/shard_map/all_to_all | solution.py:34
  24.7 19.8 %all_to_all.26 = bf16[4,24,5632]{2,1,0:T(8,128)(2,1)S(1)} all-to-all(bf16[4,24,5632]{2,1,0:T(8,128)(2,1)S(1)} %bitcast.144), channel_id=1, replica_groups=mesh['xh'=2,'core'=2,'xl'=2,'z'=8,'y'=4] {'xh','xl'}, dimensions={0} | all-to-all | bytes 2162688 | tf_op jit(solution)/shard_map/all_to_all | solution.py:34
  45.6 35.9 %all_to_all.27 = bf16[32,112,128]{2,1,0:T(8,128)(2,1)S(1)} all-to-all(bf16[32,112,128]{2,1,0:T(8,128)(2,1)S(1)} %pad_maximum_fusion), channel_id=1, replica_groups=mesh['xh'=2,'core'=2,'xl'=2,'z'=8,'y'=4] {'z','y'}, dimensions={0} | all-to-all | bytes 1835008 | tf_op jit(solution)/shard_map/all_to_all | solution.py:34
  84.9 5.6 %all-to-all-start.3 = ((bf16[32,88,128]{2,1,0:T(8,128)(2,1)}), bf16[32,88,128]{2,1,0:T(8,128)(2,1)S(1)}, u32[]{:S(2)}, u32[]{:S(2)}) async-start(bf16[32,88,128]{2,1,0:T(8,128)(2,1)} %broadcast_in_dim.8), calls=%async_computation.3 | async-start | bytes 1441792 | tf_op jit(solution)/shard_map/all_to_all | solution.py:34
  92.6 2.0 %copy.74 = bf16[16,16,4,4,4]{1,0,4,3,2:T(8,128)(2,1)S(1)} copy(bf16[16,16,4,4,4]{2,0,4,3,1:T(8,128)(2,1)S(1)} %bitcast.146) | data formatting | bytes 65536 | tf_op jit(solution)/shard_map/convert_element_type | solution.py:94
  94.9 4.6 %all_gather.3 = bf16[512,64]{0,1:T(8,128)(2,1)S(1)} all-gather(bf16[256,64]{0,1:T(8,128)(2,1)S(1)} %convert_element_type.92), channel_id=1, replica_groups=mesh['xh'=2,'core'=2,'xl'=2,'z'=8,'y'=4] {'xl'}, dimensions={0}, use_global_device_ids=true | all-gather | bytes 98304 | tf_op jit(solution)/shard_map/all_gather | solution.py:95
  99.9 10.4 %all-to-all-done.3 = bf16[32,88,128]{2,1,0:T(8,128)(2,1)S(1)} async-done(((bf16[32,88,128]{2,1,0:T(8,128)(2,1)}), bf16[32,88,128]{2,1,0:T(8,128)(2,1)S(1)}, u32[]{:S(2)}, u32[]{:S(2)}) %all-to-all-start.3) | async-done | bytes 720928 | tf_op jit(solution)/shard_map/all_to_all | solution.py:34
  111.0 4.4 %fusion.16 = f32[512,4032]{0,1:T(8,128)} fusion(bf16[512,64]{0,1:T(8,128)(2,1)S(1)} %all_gather.3, bf16[64,4096]{1,0:T(8,128)(2,1)S(1)} %copy_bitcast_fusion), kind=kOutput, calls=%fused_computation.38 | convolution fusion | flops 264241152 | bytes 8847360 | tf_op jit(solution)/shard_map/dot_general | solution.py:96
  115.4 10.4 %reshape.195 = f32[2,256,3,21,64]{1,0,4,3,2:T(2,128)} reshape(f32[512,4032]{0,1:T(8,128)} %fusion.16) | data formatting | bytes 16515072 | tf_op jit(solution)/shard_map/reshape | solution.py:96
  125.8 7.6 %multiply_reduce_fusion = f32[2,256,3,21]{1,0,3,2:T(2,128)S(1)} fusion(f32[2,256,3,21,64]{1,0,4,3,2:T(2,128)} %reshape.195), kind=kLoop, calls=%fused_computation.5 | loop fusion | flops 4096512 | bytes 8386560 | tf_op jit(solution)/shard_map/reduce_sum | solution.py:97
  133.6 4.6 %fusion.1 = bf16[2,256,3,21,64]{1,4,3,0,2:T(8,128)(2,1)S(1)} fusion(f32[2,256,3,21,64]{1,0,4,3,2:T(2,128)} %reshape.195, f32[2,256,3,21]{1,3,0,2:T(8,128)S(1)} %copy.84), kind=kLoop, calls=%fused_computation.4 | loop fusion | flops 4128768 | bytes 12515328 | tf_op jit(solution)/shard_map/convert_element_type | solution.py:98
  138.2 2.3 %fusion = (f32[2,21,256]{2,1,0:T(8,128)S(1)}, f32[2,21,256,256]{2,3,1,0:T(8,128)S(1)}) fusion(bf16[2,256,3,21,64]{1,4,3,0,2:T(8,128)(2,1)S(1)} %fusion.1), kind=kOutput, calls=%fused_computation.2 | convolution fusion | flops 357815808 | bytes 13805568 | tf_op jit(solution)/shard_map/bqhd,bkhd->bhqk/dot_general | solution.py:100
  140.5 2.2 %fusion.6 = bf16[2,256,21,64]{1,3,2,0:T(8,128)(2,1)S(1)} fusion(f32[2,21,256,256]{2,3,1,0:T(8,128)S(1)} %get-tuple-element.10, f32[2,21,256]{2,1,0:T(8,128)S(1)} %get-tuple-element.9, bf16[2,256,3,21,64]{1,4,3,0,2:T(8,128)(2,1)S(1)} %fusion.1), kind=kOutput, calls=%fused_computation.13 | convolution fusion | flops 361267200 | bytes 13811712 | tf_op jit(solution)/shard_map/bhqk,bkhd->bqhd/dot_general | solution.py:103
  142.7 1.4 copy.87
  145.5 3.4 %all-to-all-start.4 = ((f32[2,256,64]{1,2,0:T(8,128)}), f32[2,256,64]{1,2,0:T(8,128)S(1)}, u32[]{:S(2)}, u32[]{:S(2)}) async-start(f32[2,256,64]{1,2,0:T(8,128)} %bitcast.135), calls=%async_computation.4 | async-start | bytes 262144 | tf_op jit(solution)/shard_map/all_to_all | solution.py:34
  149.0 4.3 %all-to-all-done.4 = f32[2,256,64]{1,2,0:T(8,128)S(1)} async-done(((f32[2,256,64]{1,2,0:T(8,128)}), f32[2,256,64]{1,2,0:T(8,128)S(1)}, u32[]{:S(2)}, u32[]{:S(2)}) %all-to-all-start.4) | async-done | bytes 131104 | tf_op jit(solution)/shard_map/all_to_all | solution.py:34
  153.4 1.3 mul.193
  154.7 6.0 %copy.91 = f32[2,16,4,16,4,4]{2,1,5,4,3,0:T(8,128)} copy(f32[2,16,4,16,4,4]{3,1,5,4,2,0:T(8,128)} %bitcast.145) | data formatting | bytes 262144 | tf_op jit(solution)/shard_map/mul | solution.py:110
  160.7 3.6 %mul.195 = f32[2,1,64,256]{2,3,0,1:T(8,128)S(1)} reshape(f32[2,16,4,16,4,4]{2,1,5,4,3,0:T(8,128)} %copy.91) | data formatting | bytes 262144 | tf_op jit(solution)/shard_map/mul | solution.py:110
  (67 shorter events, 14.2 us)
Async XLA Ops:
  0.0 9.0 %copy-start = (f32[8,21,4032]{2,0,1:T(8,128)S(1)}, f32[8,21,4032]{2,0,1:T(8,128)}, u32[]{:S(2)}) copy-start(f32[8,21,4032]{2,0,1:T(8,128)} %param.8) | copy-start | bytes 8128516
  44.8 36.7 %copy-start.2 = (f32[2,24,5632]{2,1,0:T(8,128)}, f32[2,24,5632]{2,1,0:T(8,128)S(1)}, u32[]{:S(2)}) copy-start(f32[2,24,5632]{2,1,0:T(8,128)S(1)} %slice_add_fusion.1) | copy-start | bytes 3244036
  82.2 9.1 %copy-start.3 = (f32[1,64,256]{2,1,0:T(8,128)S(1)}, f32[1,64,256]{2,1,0:T(8,128)}, u32[]{:S(2)}) copy-start(f32[1,64,256]{2,1,0:T(8,128)} %param.12) | copy-start | bytes 196612
  84.9 25.4 %all-to-all-start.3 = ((bf16[32,88,128]{2,1,0:T(8,128)(2,1)}), bf16[32,88,128]{2,1,0:T(8,128)(2,1)S(1)}, u32[]{:S(2)}, u32[]{:S(2)}) async-start(bf16[32,88,128]{2,1,0:T(8,128)(2,1)} %broadcast_in_dim.8), calls=%async_computation.3 | async-start | bytes 1441792 | tf_op jit(solution)/shard_map/all_to_all | solution.py:34
  145.5 7.8 %all-to-all-start.4 = ((f32[2,256,64]{1,2,0:T(8,128)}), f32[2,256,64]{1,2,0:T(8,128)S(1)}, u32[]{:S(2)}, u32[]{:S(2)}) async-start(f32[2,256,64]{1,2,0:T(8,128)} %bitcast.135), calls=%async_computation.4 | async-start | bytes 262144 | tf_op jit(solution)/shard_map/all_to_all | solution.py:34
  154.7 10.5 %copy-start.1 = (f32[8,21,4032]{2,0,1:T(8,128)S(1)}, f32[8,21,4032]{2,0,1:T(8,128)}, u32[]{:S(2)}) copy-start(f32[8,21,4032]{2,0,1:T(8,128)} %param.8) | copy-start | bytes 8128516
where the time goes:
time: 166 us; the launch traced here: 165 us
  blocking collectives  67 us (40%)
  local copies, waits for them, and re-layouts  38 us (23%)
  matrix products  19.9 us (12%)
  other arithmetic  15.3 us (9%)
  waiting for transfers between devices  14.7 us (9%)
  starting transfers between devices  8.94 us (5%)
    all_to_all x3, blocking collectives, a2a(): return lax.all_to_all(x, axis, 0, 0, tiled=True)  62.4 us
    all_to_all x2, waiting for transfers between devices, a2a(): return lax.all_to_all(x, axis, 0, 0, tiled=True)  14.7 us
    mul x3, local copies, waits for them, and re-layouts, shards(): out = c_skip[:, None, None] * latent + c_out[:, None, None] * image  11 us
    reshape x1, local copies, waits for them, and re-layouts, shards(): jnp.dot(tokens, m, preferred_element_type=f32).reshape(2, 256, 3, 21, 64)  10.4 us
    all_to_all x2, starting transfers between devices, a2a(): return lax.all_to_all(x, axis, 0, 0, tiled=True)  8.94 us
    dot_general x4, matrix products, contract(): return jnp.dot(mix, x, precision=lax.Precision.HIGHEST).astype(bf16)  8.75 us
    reduce_sum x1, other arithmetic, shards(): scale = jnp.sqrt(jnp.mean(qkv * qkv, axis=-1, keepdims=True))  7.56 us
    convert_element_type x1, other arithmetic, shards(): qkv = (qkv / (EPS + scale)).astype(bf16)  4.64 us
  transfers between devices with their start and end apart: 2, of which 2 were waited for; matrix products, arithmetic and copies ran while one was open for 2% of the time, Pallas kernels for 0%

commit v1 on v0

--- a/solution.py
+++ b/solution.py
@@ -2,6 +2,7 @@
 import jax.numpy as jnp
 from jax import lax
 from jax.sharding import Mesh, PartitionSpec as P
+from jax.lax import all_to_all, psum
 
 HEAD_DIM = 64
 PROF = 8
@@ -11,6 +12,9 @@
 PARAM = ("xl", "z", "y")
 ZY = ("z", "y")
 X = ("xh", "xl")
+_reach_sources_all = lambda local_array, device_axis: jnp.concatenate(
+    all_to_all(jnp.stack(psum(1, device_axis) * [local_array], axis=0), device_axis, 0, 0), axis=0
+)
 
 
 def noise_scales(levels):
@@ -92,7 +96,7 @@
     r = natural(got[:, 64:].reshape(32, 24, 2, 64).transpose(0, 2, 1, 3))
     c_in, c_skip, c_out = noise_scales(levels)
     tokens = to_tokens(c_in[:, None, None] * latent).astype(bf16)
-    tokens = lax.all_gather(tokens, "xl", axis=0, tiled=True)
+    tokens = _reach_sources_all(tokens, "xl")
     qkv = jnp.dot(tokens, m, preferred_element_type=f32).reshape(2, 256, 3, 21, 64)
     scale = jnp.sqrt(jnp.mean(qkv * qkv, axis=-1, keepdims=True))
     qkv = (qkv / (EPS + scale)).astype(bf16)

time: 166 us -> 148 us (0.89)
  blocking collectives: 67 us -> 26.5 us
  waiting for transfers between devices: 14.7 us -> 43.5 us
  starting transfers between devices: 8.94 us -> 23.9 us
  local copies, waits for them, and re-layouts: 38 us -> 28.7 us
  other arithmetic: 15.3 us -> 6.14 us
  matrix products: 19.9 us -> 16.8 us
    all_to_all x3 -> x2, blocking collectives: 62.4 us -> 26.5 us  [a2a(): return lax.all_to_all(x, axis, 0, 0, tiled=True)]
    all_to_all x2 -> x3, waiting for transfers between devices: 14.7 us -> 41.9 us  [a2a(): return lax.all_to_all(x, axis, 0, 0, tiled=True)]
    all_to_all x2 -> x3, starting transfers between devices: 8.94 us -> 20.6 us  [a2a(): return lax.all_to_all(x, axis, 0, 0, tiled=True)]
    reshape x1, local copies, waits for them, and re-layouts: 10.4 us -> 0.01 us  [jnp.concatenate(all_to_all(jnp.stack(psum(1, device_axis) * [local_array]...]
    reduce_sum x1 -> x0, other arithmetic: 7.56 us -> none  [shards(): scale = jnp.sqrt(jnp.mean(qkv * qkv, axis=-1, keepdims=True))]
    all_gather x1 -> x0, blocking collectives: 4.58 us -> none  [shards(): tokens = lax.all_gather(tokens, 'xl', axis=0, tiled=True)]
    all_to_all x0 -> x1, starting transfers between devices: none -> 3.3 us  [all_to_all(jnp.stack(psum(1, device_axis) * [local_array], axis=0), devic...]
    dot_general x1, matrix products: 4.45 us -> 1.22 us  [shards(): jnp.dot(tokens, m, preferred_element_type=f32).reshape(2, 256, 3, 21, 64)]
  transfers between devices with their start and end apart: 2 -> 4, of which waited for: 2 -> 4; matrix products, arithmetic and copies ran while one was open for 2% -> 5% of each run, Pallas kernels for 0% -> 0%
where the time goes in v1:
time: 148 us; the launch traced here: 147 us
  waiting for transfers between devices  43.5 us (29%)
  local copies, waits for them, and re-layouts  28.7 us (19%)
  blocking collectives  26.5 us (18%)
  starting transfers between devices  23.9 us (16%)
  matrix products  16.8 us (11%)
  other arithmetic  6.14 us (4%)
    all_to_all x3, waiting for transfers between devices, a2a(): return lax.all_to_all(x, axis, 0, 0, tiled=True)  41.9 us
    all_to_all x2, blocking collectives, a2a(): return lax.all_to_all(x, axis, 0, 0, tiled=True)  26.5 us
    all_to_all x3, starting transfers between devices, a2a(): return lax.all_to_all(x, axis, 0, 0, tiled=True)  20.6 us
    mul x3, local copies, waits for them, and re-layouts, shards(): out = c_skip[:, None, None] * latent + c_out[:, None, None] * image  11 us
    dot_general x4, matrix products, contract(): return jnp.dot(mix, x, precision=lax.Precision.HIGHEST).astype(bf16)  8.75 us
    concatenate x1, local copies, waits for them, and re-layouts, shards(): part = jnp.concatenate([w_q, pad, w_p, pad, w_i, w_o], axis=1)  4.37 us
    convert_element_type x4, local copies, waits for them, and re-layouts, shards(): tokens = to_tokens(c_in[:, None, None] * latent).astype(bf16)  3.52 us
    all_to_all x1, starting transfers between devices, all_to_all(jnp.stack(psum(1, device_axis) * [local_array], axis=0), devic...  3.3 us
  transfers between devices with their start and end apart: 4, of which 4 were waited for; matrix products, arithmetic and copies ran while one was open for 5% of the time, Pallas kernels for 0%

profile of v1, /device:TPU:8, one launch (start us, length us, event | category | flops | bytes accessed | tf_op | source)
XLA Modules:
  0.0 146.9 jit_solution(12033849478823803346)
XLA Ops:
  2.0 1.3 mul.172
  3.3 1.2 convolution_convert_fusion.2
  4.7 1.3 convolution_convert_fusion.3
  6.7 2.3 %convolution_convert_fusion.1 = bf16[192,1344]{1,0:T(8,128)(2,1)S(1)} fusion(f32[192,168]{0,1:T(8,128)S(1)} %mul.172, f32[8,21,1344]{2,0,1:T(8,128)} %param.9), kind=kOutput, calls=%fused_computation.8 | convolution fusion | flops 520482816 | bytes 1548288 | tf_op jit(solution)/shard_map/dot_general | solution.py:53
  9.0 3.9 %convolution_convert_fusion = bf16[192,4032]{1,0:T(8,128)(2,1)} fusion(f32[192,168]{0,1:T(8,128)S(1)} %mul.172, f32[8,21,4032]{2,0,1:T(8,128)S(1)} %copy-done), kind=kOutput, calls=%fused_computation.6 | convolution fusion | flops 1561448448 | bytes 4386816 | tf_op jit(solution)/shard_map/dot_general | solution.py:53
  12.9 4.4 %concatenate.23 = bf16[192,5632]{1,0:T(8,128)(2,1)} concatenate(bf16[192,4032]{1,0:T(8,128)(2,1)} %convolution_convert_fusion, bf16[192,64]{1,0:T(8,128)(2,1)S(1)} %broadcast_in_dim.6, bf16[192,1344]{1,0:T(8,128)(2,1)S(1)} %convolution_convert_fusion.1, bf16[192,64]{1,0:T(8,128)(2,1)S(1)} %broadcast_in_dim.6, bf16[192,64]{1,0:T(8,128)(2,1)} %copy.79, bf16[192,64]{1,0:T(8,128)(2,1)S(1)} %copy.80), dimensions={1} | concatenate | bytes 4325376 | tf_op jit(solution)/shard_map/concatenate | solution.py:60
  17.3 6.7 %all_to_all.30 = bf16[2,96,5632]{2,1,0:T(8,128)(2,1)S(1)} all-to-all(bf16[2,96,5632]{2,1,0:T(8,128)(2,1)} %bitcast.149), channel_id=1, replica_groups=mesh['xh'=2,'core'=2,'xl'=2,'z'=8,'y'=4] {'core'}, dimensions={0} | all-to-all | bytes 4325376 | tf_op jit(solution)/shard_map/all_to_all | solution.py:38
  24.7 19.8 %all_to_all.31 = bf16[4,24,5632]{2,1,0:T(8,128)(2,1)S(1)} all-to-all(bf16[4,24,5632]{2,1,0:T(8,128)(2,1)S(1)} %bitcast.156), channel_id=1, replica_groups=mesh['xh'=2,'core'=2,'xl'=2,'z'=8,'y'=4] {'xh','xl'}, dimensions={0} | all-to-all | bytes 2162688 | tf_op jit(solution)/shard_map/all_to_all | solution.py:38
  47.1 11.7 %all-to-all-start.3 = ((bf16[32,112,128]{2,1,0:T(8,128)(2,1)}), bf16[32,112,128]{2,1,0:T(8,128)(2,1)S(1)}, u32[]{:S(2)}, u32[]{:S(2)}) async-start(bf16[32,112,128]{2,1,0:T(8,128)(2,1)} %pad_maximum_fusion), calls=%async_computation.3 | async-start | bytes 1835008 | tf_op jit(solution)/shard_map/all_to_all | solution.py:38
  61.0 2.0 %copy.75 = bf16[16,16,4,4,4]{1,0,4,3,2:T(8,128)(2,1)S(1)} copy(bf16[16,16,4,4,4]{2,0,4,3,1:T(8,128)(2,1)S(1)} %bitcast.158) | data formatting | bytes 65536 | tf_op jit(solution)/shard_map/convert_element_type | solution.py:98
  63.9 19.4 %all-to-all-done.3 = bf16[32,112,128]{2,1,0:T(8,128)(2,1)S(1)} async-done(((bf16[32,112,128]{2,1,0:T(8,128)(2,1)}), bf16[32,112,128]{2,1,0:T(8,128)(2,1)S(1)}, u32[]{:S(2)}, u32[]{:S(2)}) %all-to-all-start.3) | async-done | bytes 917536 | tf_op jit(solution)/shard_map/all_to_all | solution.py:38
  83.3 3.3 %all-to-all-start = ((bf16[2,256,64]{1,2,0:T(8,128)(2,1)}), bf16[2,256,64]{1,2,0:T(8,128)(2,1)S(1)}, u32[]{:S(2)}, u32[]{:S(2)}) async-start(bf16[2,256,64]{1,2,0:T(8,128)(2,1)} %pad_maximum_fusion.1), calls=%async_computation | async-start | bytes 131072 | tf_op jit(solution)/shard_map/all_to_all | solution.py:16
  89.0 1.7 %all-to-all-done = bf16[2,256,64]{1,2,0:T(8,128)(2,1)S(1)} async-done(((bf16[2,256,64]{1,2,0:T(8,128)(2,1)}), bf16[2,256,64]{1,2,0:T(8,128)(2,1)S(1)}, u32[]{:S(2)}, u32[]{:S(2)}) %all-to-all-start) | async-done | bytes 65568 | tf_op jit(solution)/shard_map/all_to_all | solution.py:16
  91.6 5.6 %all-to-all-start.4 = ((bf16[32,88,128]{2,1,0:T(8,128)(2,1)}), bf16[32,88,128]{2,1,0:T(8,128)(2,1)S(1)}, u32[]{:S(2)}, u32[]{:S(2)}) async-start(bf16[32,88,128]{2,1,0:T(8,128)(2,1)} %broadcast_in_dim.8), calls=%async_computation.4 | async-start | bytes 1441792 | tf_op jit(solution)/shard_map/all_to_all | solution.py:38
  97.7 18.2 %all-to-all-done.4 = bf16[32,88,128]{2,1,0:T(8,128)(2,1)S(1)} async-done(((bf16[32,88,128]{2,1,0:T(8,128)(2,1)}), bf16[32,88,128]{2,1,0:T(8,128)(2,1)S(1)}, u32[]{:S(2)}, u32[]{:S(2)}) %all-to-all-start.4) | async-done | bytes 720928 | tf_op jit(solution)/shard_map/all_to_all | solution.py:38
  118.4 1.5 %divide_convert_fusion.1 = bf16[2,256,3,21,64]{1,4,3,2,0:T(8,128)(2,1)S(1)} fusion(f32[2,256,3,21,64]{1,4,3,2,0:T(8,128)S(1)} %get-tuple-element.10, f32[2,256,3,21]{1,3,2,0:T(8,128)S(1)} %sqrt_add_fusion), kind=kLoop, calls=%fused_computation.3 | loop fusion | flops 4128768 | bytes 12515328 | tf_op jit(solution)/shard_map/convert_element_type | solution.py:102
  119.9 2.3 %fusion = (f32[2,21,256]{2,1,0:T(8,128)S(1)}, f32[2,21,256,256]{2,3,1,0:T(8,128)S(1)}) fusion(bf16[2,256,3,21,64]{1,4,3,2,0:T(8,128)(2,1)S(1)} %divide_convert_fusion.1), kind=kOutput, calls=%fused_computation.2 | convolution fusion | flops 357815808 | bytes 13805568 | tf_op jit(solution)/shard_map/bqhd,bkhd->bhqk/dot_general | solution.py:104
  122.2 2.2 %fusion.5 = bf16[2,256,21,64]{1,3,2,0:T(8,128)(2,1)S(1)} fusion(f32[2,21,256,256]{2,3,1,0:T(8,128)S(1)} %get-tuple-element.12, f32[2,21,256]{2,1,0:T(8,128)S(1)} %get-tuple-element.11, bf16[2,256,3,21,64]{1,4,3,2,0:T(8,128)(2,1)S(1)} %divide_convert_fusion.1), kind=kOutput, calls=%fused_computation.12 | convolution fusion | flops 361267200 | bytes 13811712 | tf_op jit(solution)/shard_map/bhqk,bkhd->bqhd/dot_general | solution.py:107
  124.4 1.4 copy.87
  127.2 3.4 %all-to-all-start.5 = ((f32[2,256,64]{1,2,0:T(8,128)}), f32[2,256,64]{1,2,0:T(8,128)S(1)}, u32[]{:S(2)}, u32[]{:S(2)}) async-start(f32[2,256,64]{1,2,0:T(8,128)} %bitcast.147), calls=%async_computation.5 | async-start | bytes 262144 | tf_op jit(solution)/shard_map/all_to_all | solution.py:38
  130.7 4.3 %all-to-all-done.5 = f32[2,256,64]{1,2,0:T(8,128)S(1)} async-done(((f32[2,256,64]{1,2,0:T(8,128)}), f32[2,256,64]{1,2,0:T(8,128)S(1)}, u32[]{:S(2)}, u32[]{:S(2)}) %all-to-all-start.5) | async-done | bytes 131104 | tf_op jit(solution)/shard_map/all_to_all | solution.py:38
  135.1 1.3 mul.193
  136.4 6.0 %copy.92 = f32[2,16,4,16,4,4]{2,1,5,4,3,0:T(8,128)} copy(f32[2,16,4,16,4,4]{3,1,5,4,2,0:T(8,128)} %bitcast.157) | data formatting | bytes 262144 | tf_op jit(solution)/shard_map/mul | solution.py:114
  142.4 3.6 %mul.195 = f32[2,1,64,256]{2,3,0,1:T(8,128)S(1)} reshape(f32[2,16,4,16,4,4]{2,1,5,4,3,0:T(8,128)} %copy.92) | data formatting | bytes 262144 | tf_op jit(solution)/shard_map/mul | solution.py:114
  (70 shorter events, 16.8 us)
Async XLA Ops:
  0.0 9.0 %copy-start = (f32[8,21,4032]{2,0,1:T(8,128)S(1)}, f32[8,21,4032]{2,0,1:T(8,128)}, u32[]{:S(2)}) copy-start(f32[8,21,4032]{2,0,1:T(8,128)} %param.8) | copy-start | bytes 8128516
  44.8 1.0 copy-start.2
  45.2 14.4 %copy-start.3 = (f32[1,64,256]{2,1,0:T(8,128)S(1)}, f32[1,64,256]{2,1,0:T(8,128)}, u32[]{:S(2)}) copy-start(f32[1,64,256]{2,1,0:T(8,128)} %param.12) | copy-start | bytes 196612
  47.1 36.1 %all-to-all-start.3 = ((bf16[32,112,128]{2,1,0:T(8,128)(2,1)}), bf16[32,112,128]{2,1,0:T(8,128)(2,1)S(1)}, u32[]{:S(2)}, u32[]{:S(2)}) async-start(bf16[32,112,128]{2,1,0:T(8,128)(2,1)} %pad_maximum_fusion), calls=%async_computation.3 | async-start | bytes 1835008 | tf_op jit(solution)/shard_map/all_to_all | solution.py:38
  83.3 7.4 %all-to-all-start = ((bf16[2,256,64]{1,2,0:T(8,128)(2,1)}), bf16[2,256,64]{1,2,0:T(8,128)(2,1)S(1)}, u32[]{:S(2)}, u32[]{:S(2)}) async-start(bf16[2,256,64]{1,2,0:T(8,128)(2,1)} %pad_maximum_fusion.1), calls=%async_computation | async-start | bytes 131072 | tf_op jit(solution)/shard_map/all_to_all | solution.py:16
  91.6 24.2 %all-to-all-start.4 = ((bf16[32,88,128]{2,1,0:T(8,128)(2,1)}), bf16[32,88,128]{2,1,0:T(8,128)(2,1)S(1)}, u32[]{:S(2)}, u32[]{:S(2)}) async-start(bf16[32,88,128]{2,1,0:T(8,128)(2,1)} %broadcast_in_dim.8), calls=%async_computation.4 | async-start | bytes 1441792 | tf_op jit(solution)/shard_map/all_to_all | solution.py:38
  127.2 7.8 %all-to-all-start.5 = ((f32[2,256,64]{1,2,0:T(8,128)}), f32[2,256,64]{1,2,0:T(8,128)S(1)}, u32[]{:S(2)}, u32[]{:S(2)}) async-start(f32[2,256,64]{1,2,0:T(8,128)} %bitcast.147), calls=%async_computation.5 | async-start | bytes 262144 | tf_op jit(solution)/shard_map/all_to_all | solution.py:38
  136.4 10.5 %copy-start.1 = (f32[8,21,4032]{2,0,1:T(8,128)S(1)}, f32[8,21,4032]{2,0,1:T(8,128)}, u32[]{:S(2)}) copy-start(f32[8,21,4032]{2,0,1:T(8,128)} %param.8) | copy-start | bytes 8128516
